TPU v7x, 512 devices: a whole 4x8x8 slice. The times are simulated.
512 devices in a mesh: seq: 32 (over x, y), grp: 16 (over z, core).
Axes of the slice: x: 4, y: 8, z: 8, core: 2. Of those that a mesh axis runs over, the one named last changes fastest.
Arguments:
- normed_hidden_input: bfloat16 [65536, 4096], P(('grp', 'seq')), may hold values from -6 to 6
- frozen_query_rows: bfloat16 [65536, 4096], P(('grp', 'seq')), may hold values from -16 to 16
- frozen_key_rows: bfloat16 [65536, 1024], P(('grp', 'seq')), may hold values from -16 to 16
- attention_output_gradient: bfloat16 [65536, 4096], P(('grp', 'seq')), may hold values from -0.15625 to 0.15625
- adapter_down_weight: bfloat16 [256, 64, 4096], P('grp', None, 'seq'), may hold values from -0.09375 to 0.09375
- adapter_up_weight: bfloat16 [256, 64, 1024], P('grp', 'seq'), may hold values from -0.75 to 0.75
- segment_adapter_index: int32 [16, 16], replicated, may hold values from 0 to 255, as said below
- segment_block_count: int32 [16, 16], replicated, may hold values from 1 to 16, 32 in all within a row
- adapter_row_index: int32 [256], replicated, may hold values from 0 to 255, as said below
Outputs:
- down_grad: float32 [256, 64, 4096], P('grp', None, 'seq')
- up_grad: float32 [256, 64, 1024], P('grp', 'seq')
Inputs may be any that keep to these rules, and one draw needn't show every extreme that they name: A permutation: adapter a is held in row adapter_row_index[a] of adapter_down_weight and adapter_up_weight. `segment_adapter_index`: call rows g * 16 to (g + 1) * 16 - 1 of adapter_down_weight the rows of index g of grp. In each sequence at most 2 segments use adapters held in the rows of one index of grp, and in every sequence some index holds exactly 2 of them. Tenants may repeat within and across sequences. `segment_block_count`: each row sums to 32; in each row some segment has exactly 16 blocks.
All inputs are finite; a program needn't handle non-finite values.
Results may differ from a plain program's by a relative error of at most 0.0056.
Values may be sent and summed in bfloat16 or wider, within the bound.
No kernel may reach another device: no remote copies, remote signals or barrier semaphores. Data moves between devices by JAX's collectives and lax.ppermute only.
A program may use at most 64 MiB of HBM per device.

v0:
```python
import math
import jax
import jax.numpy as jnp
from jax import lax
from jax.sharding import PartitionSpec as P

HEAD_DIM = 128
BLOCK = 128
QROWS = 512
adapter_scale = 2.0


def attend_head(query_head, key_head, grad_head, segment_ids, query_rows, reach):
    length, head_width = query_head.shape
    padded_keys = jnp.concatenate([jnp.zeros((reach, head_width), key_head.dtype), key_head], 0)
    padded_ids = jnp.concatenate([jnp.full((reach,), -1, jnp.int32), segment_ids], 0)
    window = query_rows + reach
    factor = 1.0 / math.sqrt(head_width)

    def one_block(totals, number):
        offset = number * query_rows
        query_block = lax.dynamic_slice_in_dim(query_head, offset, query_rows, 0)
        grad_block = lax.dynamic_slice_in_dim(grad_head, offset, query_rows, 0)
        key_block = lax.dynamic_slice_in_dim(padded_keys, offset, window, 0)
        key_ids = lax.dynamic_slice_in_dim(padded_ids, offset, window, 0)
        query_ids = lax.dynamic_slice_in_dim(segment_ids, offset, query_rows, 0)
        scores = jnp.dot(query_block, key_block.T, preferred_element_type=jnp.float32) * factor
        query_pos = offset + jnp.arange(query_rows, dtype=jnp.int32)
        key_pos = offset - reach + jnp.arange(window, dtype=jnp.int32)
        allowed = (key_ids[None, :] == query_ids[:, None]) & (
            key_pos[None, :] <= query_pos[:, None]
        )
        scores = jnp.where(allowed, scores, jnp.float32(-1e30))
        highest = jnp.max(scores, axis=1, keepdims=True)
        expo = jnp.exp(scores - highest)
        probabilities = (expo / jnp.sum(expo, axis=1, keepdims=True)).astype(jnp.bfloat16)
        contribution = jnp.dot(probabilities.T, grad_block, preferred_element_type=jnp.float32)
        current = lax.dynamic_slice_in_dim(totals, offset, window, 0)
        totals = lax.dynamic_update_slice_in_dim(totals, current + contribution, offset, 0)
        return (totals, None)

    initial = jnp.zeros((length + reach, head_width), jnp.float32)
    totals, _ = lax.scan(one_block, initial, jnp.arange(length // query_rows, dtype=jnp.int32))
    return totals[reach:].astype(jnp.bfloat16)


def local(
    normed_hidden_input,
    frozen_query_rows,
    frozen_key_rows,
    attention_output_gradient,
    adapter_down_weight,
    adapter_up_weight,
    segment_adapter_index,
    segment_block_count,
    adapter_row_index,
):
    group_count = lax.axis_size("grp")
    shard_count = lax.axis_size("seq")
    group_index = lax.axis_index("grp")
    tokens_here, model_width = normed_hidden_input.shape
    portion_width = adapter_down_weight.shape[2]
    resident_adapters, rank_overall = (adapter_down_weight.shape[0], adapter_down_weight.shape[1])
    rank_portion, value_projection_width = (adapter_up_weight.shape[1], adapter_up_weight.shape[2])
    segments = segment_adapter_index.shape[1]
    capacity = max(2, (segments + group_count - 1) // group_count)
    seq_length = tokens_here * shard_count
    block_total = seq_length // BLOCK
    block_here = tokens_here // BLOCK
    reach = min(16, seq_length // (2 * BLOCK)) * BLOCK
    head_total = frozen_query_rows.shape[1] // HEAD_DIM
    kv_heads = value_projection_width // HEAD_DIM
    heads_here = head_total // shard_count
    group_size = head_total // kv_heads
    slot_total = group_count * capacity
    adapter_ids = jnp.arange(adapter_row_index.shape[0], dtype=jnp.int32)
    slot_of = jnp.sum(
        jnp.where(segment_adapter_index[:, :, None] == adapter_ids, adapter_row_index, 0), axis=2
    )
    owner_group = slot_of // resident_adapters
    local_slot = slot_of % resident_adapters
    order_ids = jnp.arange(segments, dtype=jnp.int32)
    earlier = order_ids[:, None] > order_ids[None, :]
    same_owner = owner_group[:, :, None] == owner_group[:, None, :]
    rank_in_owner = jnp.sum((same_owner & earlier[None]).astype(jnp.int32), axis=2)
    placement = owner_group * capacity + rank_in_owner
    capacity_ids = jnp.arange(capacity, dtype=jnp.int32)
    local_ids = jnp.arange(resident_adapters, dtype=jnp.int32)
    picks = (
        (owner_group == group_index)[:, :, None, None]
        & (rank_in_owner[:, :, None, None] == capacity_ids[:, None])
        & (local_slot[:, :, None, None] == local_ids)
    )
    chooser = jnp.sum(picks.astype(jnp.float32), axis=1)
    selector_half = chooser.astype(jnp.bfloat16)
    send_down = jnp.einsum(
        "pgl,lut->pgut", selector_half, adapter_down_weight, preferred_element_type=jnp.float32
    ).astype(jnp.bfloat16)
    send_up = jnp.einsum(
        "gyv,vmf->gymf", selector_half, adapter_up_weight, preferred_element_type=jnp.float32
    ).astype(jnp.bfloat16)
    fetched_down, fetched_up = (
        lax.all_to_all(send_down, "grp", split_axis=0, concat_axis=0, tiled=True),
        lax.all_to_all(send_up, "grp", split_axis=0, concat_axis=0, tiled=True),
    )
    own_blocks = segment_block_count[group_index]
    ends = jnp.cumsum(own_blocks)
    block_seg = jnp.sum(
        (jnp.arange(block_total, dtype=jnp.int32)[:, None] >= ends[None, :]).astype(jnp.int32),
        axis=1,
    )
    own_place = placement[group_index]
    block_place = jnp.sum(
        jnp.where(block_seg[:, None] == order_ids[None, :], own_place[None, :], 0), axis=1
    )
    block_pick = block_place[:, None] == jnp.arange(slot_total, dtype=jnp.int32)[None, :]
    pick_half = block_pick.astype(jnp.bfloat16)
    segment_ids = jnp.broadcast_to(block_seg[:, None], (block_total, BLOCK)).reshape(seq_length)
    block_down_weight = jnp.einsum(
        "bn,nrd->brd",
        pick_half,
        fetched_down.reshape(slot_total, rank_overall, portion_width),
        preferred_element_type=jnp.float32,
    ).astype(jnp.bfloat16)
    block_up_rows = jnp.einsum(
        "bn,nre->bre",
        pick_half,
        fetched_up.reshape(slot_total, rank_portion, value_projection_width),
        preferred_element_type=jnp.float32,
    ).astype(jnp.bfloat16)
    features = lax.all_to_all(normed_hidden_input, "seq", split_axis=1, concat_axis=0, tiled=True)
    amount = lax.axis_size("seq") * tokens_here
    token_rows = features.reshape(amount // BLOCK, BLOCK, portion_width)
    reduced_rank_part = (
        lax.psum_scatter(
            jnp.einsum(
                "jyw,jaw->jya", token_rows, block_down_weight, preferred_element_type=jnp.float32
            ).reshape(amount, rank_overall),
            "seq",
            scatter_dimension=0,
            tiled=True,
        )
        .astype(jnp.bfloat16)
        .reshape(block_here, BLOCK, rank_overall)
    )
    near_up = lax.all_to_all(block_up_rows, "seq", split_axis=0, concat_axis=1, tiled=True)
    query_grid = frozen_query_rows.reshape(tokens_here, shard_count, heads_here, HEAD_DIM)
    key_grid = jnp.repeat(
        frozen_key_rows.reshape(tokens_here, kv_heads, HEAD_DIM), group_size, axis=1
    ).reshape(tokens_here, shard_count, heads_here, HEAD_DIM)
    grad_grid = attention_output_gradient.reshape(tokens_here, shard_count, heads_here, HEAD_DIM)
    query_all = lax.all_to_all(query_grid, "seq", split_axis=1, concat_axis=0, tiled=True)
    key_all = lax.all_to_all(key_grid, "seq", split_axis=1, concat_axis=0, tiled=True)
    grad_all = lax.all_to_all(grad_grid, "seq", split_axis=1, concat_axis=0, tiled=True)

    def per_head(triple):
        return attend_head(triple[0], triple[1], triple[2], segment_ids, QROWS, reach)

    stacked = (
        jnp.moveaxis(query_all[:, 0], 1, 0),
        jnp.moveaxis(key_all[:, 0], 1, 0),
        jnp.moveaxis(grad_all[:, 0], 1, 0),
    )
    result = lax.map(per_head, stacked)
    head_grads = jnp.moveaxis(result, 0, 1)[:, None]
    token_grads = lax.all_to_all(head_grads, "seq", split_axis=0, concat_axis=1, tiled=True)
    value_grad = jnp.sum(
        token_grads.reshape(tokens_here, kv_heads, group_size, HEAD_DIM), axis=2, dtype=jnp.float32
    )
    value_row_blocks = value_grad.reshape(block_here, BLOCK, value_projection_width).astype(
        jnp.bfloat16
    )
    up_weight_terms = adapter_scale * jnp.einsum(
        "fvg,fvn->fgn", reduced_rank_part, value_row_blocks, preferred_element_type=jnp.float32
    )
    backward_rank_part = (
        adapter_scale
        * jnp.einsum("vaw,vpw->vap", value_row_blocks, near_up, preferred_element_type=jnp.float32)
    ).astype(jnp.bfloat16)
    all_low = lax.all_gather(
        backward_rank_part.reshape(tokens_here, rank_overall), "seq", axis=0, tiled=True
    )
    back_down = jnp.einsum(
        "jcy,jct->jyt",
        all_low.reshape(block_total, BLOCK, rank_overall),
        features.reshape(block_total, BLOCK, portion_width),
        preferred_element_type=jnp.float32,
    )
    back_up = lax.all_to_all(up_weight_terms, "seq", split_axis=1, concat_axis=0, tiled=True)
    pick_full = block_pick.astype(jnp.float32)
    slot_down = jnp.einsum("bn,brd->nrd", pick_full, back_down, precision=lax.Precision.HIGHEST)
    slot_up = jnp.einsum("bn,bre->nre", pick_full, back_up, precision=lax.Precision.HIGHEST)
    return_down, return_up = (
        lax.all_to_all(
            slot_down.reshape(group_count, capacity, rank_overall, portion_width),
            "grp",
            split_axis=0,
            concat_axis=0,
            tiled=True,
        ),
        lax.all_to_all(
            slot_up.reshape(group_count, capacity, rank_portion, value_projection_width),
            "grp",
            split_axis=0,
            concat_axis=0,
            tiled=True,
        ),
    )
    down_grad = jnp.einsum("nca,ncrd->ard", chooser, return_down, precision=lax.Precision.HIGHEST)
    up_grad = jnp.einsum("nca,ncre->are", chooser, return_up, precision=lax.Precision.HIGHEST)
    return (down_grad, up_grad)


def solution(mesh):
    return jax.shard_map(
        local,
        mesh=mesh,
        in_specs=(
            P(("grp", "seq"), None),
            P(("grp", "seq"), None),
            P(("grp", "seq"), None),
            P(("grp", "seq"), None),
            P("grp", None, "seq"),
            P("grp", "seq", None),
            P(),
            P(),
            P(),
        ),
        out_specs=(P("grp", None, "seq"), P("grp", "seq", None)),
        check_vma=False,
    )
```

profile of v0, /device:TPU:1, one launch (start us, length us, event | category | flops | bytes accessed | tf_op | source)
XLA Modules:
  0.0 591.7 jit_solution(1120349917430718640)
XLA Ops:
  7.2 1.2 select_reduce_fusion
  9.2 1.0 convolution_convert_fusion.3
  11.0 11.8 %all-to-all-start.4 = ((bf16[16,2,2,1024]{3,2,1,0:T(2,128)(2,1)}), bf16[16,2,2,1024]{3,2,1,0:T(2,128)(2,1)S(1)}, u32[]{:S(2)}, u32[]{:S(2)}) async-start(bf16[16,2,2,1024]{3,2,1,0:T(2,128)(2,1)} %copy.109), calls=%async_computation.4 | async-start | bytes 262144 | tf_op jit(solution)/shard_map/all_to_all | solution.py:104
  22.8 1.2 convolution_convert_fusion.1
  25.0 7.0 %all-to-all-done.4 = bf16[16,2,2,1024]{3,2,1,0:T(2,128)(2,1)S(1)} async-done(((bf16[16,2,2,1024]{3,2,1,0:T(2,128)(2,1)}), bf16[16,2,2,1024]{3,2,1,0:T(2,128)(2,1)S(1)}, u32[]{:S(2)}, u32[]{:S(2)}) %all-to-all-start.4) | async-done | bytes 131104 | tf_op jit(solution)/shard_map/all_to_all | solution.py:104
  32.0 3.5 all-to-all-start.8
  35.5 16.8 %all-to-all-done.8 = bf16[16,2,64,128]{3,2,1,0:T(8,128)(2,1)S(1)} async-done(((bf16[16,2,64,128]{3,2,1,0:T(8,128)(2,1)}), bf16[16,2,64,128]{3,2,1,0:T(8,128)(2,1)S(1)}, u32[]{:S(2)}, u32[]{:S(2)}) %all-to-all-start.8) | async-done | bytes 524320 | tf_op jit(solution)/shard_map/all_to_all | solution.py:103
  52.3 1.2 broadcast_in_dim.41
  53.5 9.7 %all-to-all-start.1 = ((bf16[128,32,1,128]{3,0,2,1:T(8,128)(2,1)}), bf16[128,32,1,128]{3,0,2,1:T(8,128)(2,1)S(1)}, u32[]{:S(2)}, u32[]{:S(2)}) async-start(bf16[128,32,1,128]{3,0,2,1:T(8,128)(2,1)} %bitcast.10), calls=%async_computation.1 | async-start | bytes 2097152 | tf_op jit(solution)/shard_map/all_to_all | solution.py:153
  63.2 1.6 copy.103
  64.8 1.3 copy.104
  66.2 25.2 %all-to-all-done.1 = bf16[128,32,1,128]{3,0,2,1:T(8,128)(2,1)S(1)} async-done(((bf16[128,32,1,128]{3,0,2,1:T(8,128)(2,1)}), bf16[128,32,1,128]{3,0,2,1:T(8,128)(2,1)S(1)}, u32[]{:S(2)}, u32[]{:S(2)}) %all-to-all-start.1) | async-done | bytes 1048608 | tf_op jit(solution)/shard_map/all_to_all | solution.py:153
  91.4 5.6 all-to-all-start.2
  97.0 1.6 copy.100
  98.6 1.3 copy.101
  99.9 22.2 %all-to-all-done.2 = bf16[128,32,1,128]{3,0,2,1:T(8,128)(2,1)} async-done(((bf16[128,32,1,128]{3,0,2,1:T(8,128)(2,1)}), bf16[128,32,1,128]{3,0,2,1:T(8,128)(2,1)}, u32[]{:S(2)}, u32[]{:S(2)}) %all-to-all-start.2) | async-done | bytes 1048608 | tf_op jit(solution)/shard_map/all_to_all | solution.py:154
  122.2 8.1 %all-to-all-start = ((bf16[128,32,1,128]{3,0,2,1:T(8,128)(2,1)}), bf16[128,32,1,128]{3,0,2,1:T(8,128)(2,1)}, u32[]{:S(2)}, u32[]{:S(2)}) async-start(bf16[128,32,1,128]{3,0,2,1:T(8,128)(2,1)} %copy.101), calls=%async_computation | async-start | bytes 2097152 | tf_op jit(solution)/shard_map/all_to_all | solution.py:152
  131.2 1.6 copy.112
  132.8 1.3 copy.113
  134.4 1.2 convolution_convert_fusion
  135.8 19.1 %all-to-all-done = bf16[128,32,1,128]{3,0,2,1:T(8,128)(2,1)} async-done(((bf16[128,32,1,128]{3,0,2,1:T(8,128)(2,1)}), bf16[128,32,1,128]{3,0,2,1:T(8,128)(2,1)}, u32[]{:S(2)}, u32[]{:S(2)}) %all-to-all-start) | async-done | bytes 1048608 | tf_op jit(solution)/shard_map/all_to_all | solution.py:152
  154.9 8.6 %all-to-all-start.6 = ((bf16[128,32,128]{2,0,1:T(8,128)(2,1)}), bf16[128,32,128]{2,0,1:T(8,128)(2,1)S(1)}, u32[]{:S(2)}, u32[]{:S(2)}) async-start(bf16[128,32,128]{2,0,1:T(8,128)(2,1)} %copy.113), calls=%async_computation.6 | async-start | bytes 2097152 | tf_op jit(solution)/shard_map/all_to_all | solution.py:131
  163.5 1.9 broadcast.202
  165.3 67.9 %while.19 = (s32[]{:T(128)}, f32[6144,128]{1,0:T(8,128)}, s32[8]{0:T(128)S(1)}, s32[6144]{0:T(1024)S(1)}, s32[4096]{0:T(1024)S(1)}, /*index=5*/bf16[4096,128]{1,...) while((s32[]{:T(128)}, f32[6144,128]{1,0:T(8,128)}, ...), condition=%wide.region_9.10_spmd, body=%wide.region_6.9_spmd.sunk | while | flops 685836288 | bytes 19343620 | solution.py:43
  166.8 2.4 fusion.62
  170.0 3.8 fusion.64
  175.2 2.4 fusion.62
  178.5 3.8 fusion.64
  183.7 2.4 fusion.62
  187.0 3.8 fusion.64
  192.2 2.4 fusion.62
  195.5 3.8 fusion.64
  200.7 2.4 fusion.62
  204.0 3.8 fusion.64
  209.2 2.4 fusion.62
  212.5 3.8 fusion.64
  217.7 2.4 fusion.62
  221.0 3.8 fusion.64
  226.2 2.4 fusion.62
  229.5 3.8 fusion.64
  233.3 1.7 fusion.9
  235.5 1.4 reduce.3
  236.9 1.2 reshape.260
  238.1 9.2 %all-to-all-start.3 = ((bf16[32,2,8192]{2,1,0:T(2,128)(2,1)}), bf16[32,2,8192]{2,1,0:T(2,128)(2,1)S(1)}, u32[]{:S(2)}, u32[]{:S(2)}) async-start(bf16[32,2,8192]{2,1,0:T(2,128)(2,1)} %reshape.260), calls=%async_computation.3 | async-start | bytes 2097152 | tf_op jit(solution)/shard_map/all_to_all | solution.py:166
  247.6 1.9 convolution_bitcast_fusion
  249.4 1.1 copy.185
  251.6 20.3 %all-to-all-done.3 = bf16[32,2,8192]{2,1,0:T(2,128)(2,1)S(1)} async-done(((bf16[32,2,8192]{2,1,0:T(2,128)(2,1)}), bf16[32,2,8192]{2,1,0:T(2,128)(2,1)S(1)}, u32[]{:S(2)}, u32[]{:S(2)}) %all-to-all-start.3) | async-done | bytes 1048608 | tf_op jit(solution)/shard_map/all_to_all | solution.py:166
  271.9 1.0 copy-done.1
  272.9 8.3 %all-to-all-start.5 = ((bf16[32,2,1024]{2,1,0:T(2,128)(2,1)}), bf16[32,2,1024]{2,1,0:T(2,128)(2,1)S(1)}, u32[]{:S(2)}, u32[]{:S(2)}) async-start(bf16[32,2,1024]{2,1,0:T(2,128)(2,1)} %copy.111), calls=%async_computation.5 | async-start | bytes 262144 | tf_op jit(solution)/shard_map/all_to_all | solution.py:146
  281.3 4.3 reshape.261
  285.6 1.2 copy.146
  286.7 1.4 reduce_sum.74
  288.3 176.5 %reduce-scatter.2.cloned.1.call-done = f32[128,64]{0,1:T(8,128)} async-done(((f32[4096,64]{0,1:T(8,128)}), f32[128,64]{0,1:T(8,128)}) %reduce-scatter.2.cloned.1.call-update) | async-done | bytes 32784 | tf_op jit(solution)/shard_map/reduce_scatter | solution.py:135
  464.8 1.0 fusion.7
  465.8 1.0 copy.126
  466.8 6.5 %all-to-all-start.9 = ((f32[1,64,1024]{2,0,1:T(1,128)}), f32[1,64,1024]{2,0,1:T(1,128)S(1)}, u32[]{:S(2)}, u32[]{:S(2)}) async-start(f32[1,64,1024]{2,0,1:T(1,128)} %copy.126), calls=%async_computation.10 | async-start | bytes 524288 | tf_op jit(solution)/shard_map/all_to_all | solution.py:189
  473.5 39.6 %all_gather.3 = bf16[4096,64]{0,1:T(8,128)(2,1)S(1)} all-gather(bf16[128,64]{0,1:T(8,128)(2,1)S(1)} %fusion.8), channel_id=1, replica_groups=mesh['seq'=32,'grp'=16] {'seq'}, dimensions={0}, use_global_device_ids=true | all-gather | bytes 540672 | tf_op jit(solution)/shard_map/all_gather | solution.py:180
  515.2 25.0 %all-to-all-start.10 = ((f32[16,2,2,1024]{3,1,2,0:T(2,128)}), f32[16,2,2,1024]{3,1,2,0:T(2,128)S(1)}, u32[]{:S(2)}, u32[]{:S(2)}) async-start(f32[16,2,2,1024]{3,1,2,0:T(2,128)} %copy.128), calls=%async_computation.11 | async-start | bytes 524288 | tf_op jit(solution)/shard_map/all_to_all | solution.py:201
  540.6 1.3 fusion.14
  541.9 1.5 copy.117
  543.5 8.4 %all-to-all-done.10 = f32[16,2,2,1024]{3,1,2,0:T(2,128)S(1)} async-done(((f32[16,2,2,1024]{3,1,2,0:T(2,128)}), f32[16,2,2,1024]{3,1,2,0:T(2,128)S(1)}, u32[]{:S(2)}, u32[]{:S(2)}) %all-to-all-start.10) | async-done | bytes 262176 | tf_op jit(solution)/shard_map/all_to_all | solution.py:201
  551.9 3.6 all-to-all-start.7
  556.7 26.0 %all-to-all-done.7 = f32[16,2,64,128]{3,1,2,0:T(2,128)S(1)} async-done(((f32[16,2,64,128]{3,1,2,0:T(2,128)}), f32[16,2,64,128]{3,1,2,0:T(2,128)S(1)}, u32[]{:S(2)}, u32[]{:S(2)}) %all-to-all-start.7) | async-done | bytes 1048608 | tf_op jit(solution)/shard_map/all_to_all | solution.py:194
  582.7 1.2 convolution_bitcast_fusion.1
  (99 shorter events, 23.6 us)
Async XLA Ops:
  7.2 28.3 %copy-start = (bf16[128,1024]{1,0:T(8,128)(2,1)S(1)}, bf16[128,1024]{1,0:T(8,128)(2,1)}, u32[]{:S(2)}) copy-start(bf16[128,1024]{1,0:T(8,128)(2,1)} %param.13) | copy-start | bytes 786436
  11.0 21.0 %all-to-all-start.4 = ((bf16[16,2,2,1024]{3,2,1,0:T(2,128)(2,1)}), bf16[16,2,2,1024]{3,2,1,0:T(2,128)(2,1)S(1)}, u32[]{:S(2)}, u32[]{:S(2)}) async-start(bf16[16,2,2,1024]{3,2,1,0:T(2,128)(2,1)} %copy.109), calls=%async_computation.4 | async-start | bytes 262144 | tf_op jit(solution)/shard_map/all_to_all | solution.py:104
  32.0 20.3 %all-to-all-start.8 = ((bf16[16,2,64,128]{3,2,1,0:T(8,128)(2,1)}), bf16[16,2,64,128]{3,2,1,0:T(8,128)(2,1)S(1)}, u32[]{:S(2)}, u32[]{:S(2)}) async-start(bf16[16,2,64,128]{3,2,1,0:T(8,128)(2,1)} %copy.122), calls=%async_computation.8 | async-start | bytes 1048576 | tf_op jit(solution)/shard_map/all_to_all | solution.py:103
  53.5 37.9 %all-to-all-start.1 = ((bf16[128,32,1,128]{3,0,2,1:T(8,128)(2,1)}), bf16[128,32,1,128]{3,0,2,1:T(8,128)(2,1)S(1)}, u32[]{:S(2)}, u32[]{:S(2)}) async-start(bf16[128,32,1,128]{3,0,2,1:T(8,128)(2,1)} %bitcast.10), calls=%async_computation.1 | async-start | bytes 2097152 | tf_op jit(solution)/shard_map/all_to_all | solution.py:153
  91.4 30.8 %all-to-all-start.2 = ((bf16[128,32,1,128]{3,0,2,1:T(8,128)(2,1)}), bf16[128,32,1,128]{3,0,2,1:T(8,128)(2,1)}, u32[]{:S(2)}, u32[]{:S(2)}) async-start(bf16[128,32,1,128]{3,0,2,1:T(8,128)(2,1)} %copy.104), calls=%async_computation.2 | async-start | bytes 2097152 | tf_op jit(solution)/shard_map/all_to_all | solution.py:154
  122.2 32.7 %all-to-all-start = ((bf16[128,32,1,128]{3,0,2,1:T(8,128)(2,1)}), bf16[128,32,1,128]{3,0,2,1:T(8,128)(2,1)}, u32[]{:S(2)}, u32[]{:S(2)}) async-start(bf16[128,32,1,128]{3,0,2,1:T(8,128)(2,1)} %copy.101), calls=%async_computation | async-start | bytes 2097152 | tf_op jit(solution)/shard_map/all_to_all | solution.py:152
  134.4 30.9 %copy-start.2 = (s32[32]{0:T(128)}, s32[32]{0:T(128)S(1)}, u32[]{:S(2)}) copy-start(s32[32]{0:T(128)S(1)} %select_reduce_fusion.1) | copy-start | bytes 388
  154.9 83.2 %all-to-all-start.6 = ((bf16[128,32,128]{2,0,1:T(8,128)(2,1)}), bf16[128,32,128]{2,0,1:T(8,128)(2,1)S(1)}, u32[]{:S(2)}, u32[]{:S(2)}) async-start(bf16[128,32,128]{2,0,1:T(8,128)(2,1)} %copy.113), calls=%async_computation.6 | async-start | bytes 2097152 | tf_op jit(solution)/shard_map/all_to_all | solution.py:131
  238.1 12.4 %copy-start.3 = (s32[32]{0:T(128)S(1)}, s32[32]{0:T(128)}, u32[]{:S(2)}) copy-start(s32[32]{0:T(128)} %copy-done.2) | copy-start | bytes 388
  238.1 33.8 %all-to-all-start.3 = ((bf16[32,2,8192]{2,1,0:T(2,128)(2,1)}), bf16[32,2,8192]{2,1,0:T(2,128)(2,1)S(1)}, u32[]{:S(2)}, u32[]{:S(2)}) async-start(bf16[32,2,8192]{2,1,0:T(2,128)(2,1)} %reshape.260), calls=%async_computation.3 | async-start | bytes 2097152 | tf_op jit(solution)/shard_map/all_to_all | solution.py:166
  247.4 217.5 %reduce-scatter.2.cloned.1.call-start = ((), (), s32[]{:S(2)}) async-start(), calls=%async_computation.12 | async-start | bytes 1081344 | tf_op jit(solution)/shard_map/reduce_scatter | solution.py:135
  271.9 1.0 copy-start.1
  272.9 193.9 %all-to-all-start.5 = ((bf16[32,2,1024]{2,1,0:T(2,128)(2,1)}), bf16[32,2,1024]{2,1,0:T(2,128)(2,1)S(1)}, u32[]{:S(2)}, u32[]{:S(2)}) async-start(bf16[32,2,1024]{2,1,0:T(2,128)(2,1)} %copy.111), calls=%async_computation.5 | async-start | bytes 262144 | tf_op jit(solution)/shard_map/all_to_all | solution.py:146
  286.7 227.2 %copy-start.4 = (s32[32]{0:T(128)S(1)}, s32[32]{0:T(128)}, u32[]{:S(2)}) copy-start(s32[32]{0:T(128)} %copy-done.2) | copy-start | bytes 388
  466.8 46.3 %all-to-all-start.9 = ((f32[1,64,1024]{2,0,1:T(1,128)}), f32[1,64,1024]{2,0,1:T(1,128)S(1)}, u32[]{:S(2)}, u32[]{:S(2)}) async-start(f32[1,64,1024]{2,0,1:T(1,128)} %copy.126), calls=%async_computation.10 | async-start | bytes 524288 | tf_op jit(solution)/shard_map/all_to_all | solution.py:189
  515.2 36.7 %all-to-all-start.10 = ((f32[16,2,2,1024]{3,1,2,0:T(2,128)}), f32[16,2,2,1024]{3,1,2,0:T(2,128)S(1)}, u32[]{:S(2)}, u32[]{:S(2)}) async-start(f32[16,2,2,1024]{3,1,2,0:T(2,128)} %copy.128), calls=%async_computation.11 | async-start | bytes 524288 | tf_op jit(solution)/shard_map/all_to_all | solution.py:201
  551.9 30.8 %all-to-all-start.7 = ((f32[16,2,64,128]{3,1,2,0:T(2,128)}), f32[16,2,64,128]{3,1,2,0:T(2,128)S(1)}, u32[]{:S(2)}, u32[]{:S(2)}) async-start(f32[16,2,64,128]{3,1,2,0:T(2,128)} %copy.117), calls=%async_computation.7 | async-start | bytes 2097152 | tf_op jit(solution)/shard_map/all_to_all | solution.py:194
Sparse Core Ops, SparseCore 0:
  252.6 212.2 reduce-scatter.1
where the time goes:
time: 594 us; the launch traced here: 592 us
  waiting for transfers between devices  322 us (54%)
  starting transfers between devices  100 us (17%)
  matrix products  60.2 us (10%)
  blocking collectives  39.6 us (7%)
  local copies, waits for them, and re-layouts  38.2 us (6%)
  between operations  14.4 us (2%)
  other arithmetic  12.6 us (2%)
    reduce_scatter x1, waiting for transfers between devices, local(): lax.psum_scatter(jnp.einsum('jyw,jaw->jya', token_rows, block_down_weight...  177 us
    all_gather x1, blocking collectives, local(): lax.all_gather(backward_rank_part.reshape(tokens_here, rank_overall), 'se...  39.6 us
    dot_general x8, matrix products, one_block(): jnp.dot(probabilities.T, grad_block, preferred_element_type=jnp.float32)  30.3 us
    all_to_all x1, waiting for transfers between devices, local(): lax.all_to_all(slot_down.reshape(group_count, capacity, rank_overall, por...  26 us
    all_to_all x1, waiting for transfers between devices, local(): lax.all_to_all(key_grid, 'seq', split_axis=1, concat_axis=0, tiled=True)  25.2 us
    all_to_all x1, starting transfers between devices, local(): lax.all_to_all(slot_up.reshape(group_count, capacity, rank_portion, value...  25 us
    all_to_all x1, waiting for transfers between devices, local(): lax.all_to_all(grad_grid, 'seq', split_axis=1, concat_axis=0, tiled=True)  22.2 us
    all_to_all x1, waiting for transfers between devices, local(): lax.all_to_all(head_grads, 'seq', split_axis=0, concat_axis=1, tiled=True)  20.3 us
  transfers between devices with their start and end apart: 12, of which 9 were waited for; matrix products, arithmetic and copies ran while one was open for 17% of the time, Pallas kernels for 0%

commit v1 on v0

--- a/solution.py
+++ b/solution.py
@@ -177,9 +177,9 @@
         adapter_scale
         * jnp.einsum("vaw,vpw->vap", value_row_blocks, near_up, preferred_element_type=jnp.float32)
     ).astype(jnp.bfloat16)
-    all_low = lax.all_gather(
-        backward_rank_part.reshape(tokens_here, rank_overall), "seq", axis=0, tiled=True
-    )
+    block = backward_rank_part.reshape(tokens_here, rank_overall)
+    stack = jnp.stack([block] * lax.axis_size("seq"))
+    all_low = jnp.concatenate(lax.all_to_all(stack, "seq", 0, 0), axis=0)
     back_down = jnp.einsum(
         "jcy,jct->jyt",
         all_low.reshape(block_total, BLOCK, rank_overall),

time: 594 us -> 574 us (0.966)
  blocking collectives: 39.6 us -> 0 us
  waiting for transfers between devices: 322 us -> 340 us
  local copies, waits for them, and re-layouts: 38.2 us -> 52.6 us
  matrix products: 60.2 us -> 50.9 us
    all_gather x1 -> x0, blocking collectives: 39.6 us -> none  [local(): lax.all_gather(backward_rank_part.reshape(tokens_here, rank_overall), 'se...]
    while x0 -> x32, local copies, waits for them, and re-layouts: none -> 13.3 us
    dot_general x8, matrix products: 30.3 us -> 19.9 us  [one_block(): jnp.dot(probabilities.T, grad_block, preferred_element_type=jnp.float32)]
    all_to_all x1, waiting for transfers between devices: 0.01 us -> 9.41 us  [local(): lax.all_to_all(up_weight_terms, 'seq', split_axis=1, concat_axis=0, tiled...]
    all_to_all x0 -> x1, waiting for transfers between devices: none -> 9.32 us  [local(): all_low = jnp.concatenate(lax.all_to_all(stack, 'seq', 0, 0), axis=0)]
    all_to_all x1, waiting for transfers between devices: 19.1 us -> 28.1 us  [local(): lax.all_to_all(query_grid, 'seq', split_axis=1, concat_axis=0, tiled=True)]
    all_to_all x1, starting transfers between devices: 25 us -> 16.1 us  [local(): lax.all_to_all(slot_up.reshape(group_count, capacity, rank_portion, value...]
    unnamed x18 -> x20, local copies, waits for them, and re-layouts: 14.3 us -> 14.3 us
  transfers between devices with their start and end apart: 12 -> 13, of which waited for: 9 -> 11; matrix products, arithmetic and copies ran while one was open for 17% -> 16% of each run, Pallas kernels for 0% -> 0%
where the time goes in v1:
time: 574 us; the launch traced here: 572 us
  waiting for transfers between devices  340 us (59%)
  starting transfers between devices  95.5 us (17%)
  local copies, waits for them, and re-layouts  52.6 us (9%)
  matrix products  50.9 us (9%)
  between operations  14.4 us (3%)
  other arithmetic  12.6 us (2%)
    reduce_scatter x1, waiting for transfers between devices, local(): lax.psum_scatter(jnp.einsum('jyw,jaw->jya', token_rows, block_down_weight...  176 us
    all_to_all x1, waiting for transfers between devices, local(): lax.all_to_all(query_grid, 'seq', split_axis=1, concat_axis=0, tiled=True)  28.1 us
    all_to_all x1, waiting for transfers between devices, local(): lax.all_to_all(slot_down.reshape(group_count, capacity, rank_overall, por...  26 us
    all_to_all x1, waiting for transfers between devices, local(): lax.all_to_all(key_grid, 'seq', split_axis=1, concat_axis=0, tiled=True)  22.3 us
    dot_general x8, matrix products, one_block(): jnp.dot(query_block, key_block.T, preferred_element_type=jnp.float32)  20.7 us
    all_to_all x1, waiting for transfers between devices, local(): lax.all_to_all(head_grads, 'seq', split_axis=0, concat_axis=1, tiled=True)  20.3 us
    dot_general x8, matrix products, one_block(): jnp.dot(probabilities.T, grad_block, preferred_element_type=jnp.float32)  19.9 us
    all_to_all x1, waiting for transfers between devices, local(): lax.all_to_all(grad_grid, 'seq', split_axis=1, concat_axis=0, tiled=True)  19.1 us
  transfers between devices with their start and end apart: 13, of which 11 were waited for; matrix products, arithmetic and copies ran while one was open for 16% of the time, Pallas kernels for 0%

profile of v1, /device:TPU:1, one launch (start us, length us, event | category | flops | bytes accessed | tf_op | source)
XLA Modules:
  0.0 571.7 jit_solution(17796660449488075796)
XLA Ops:
  11.0 11.8 %all-to-all-start.4 = ((bf16[16,2,2,1024]{3,2,1,0:T(2,128)(2,1)}), bf16[16,2,2,1024]{3,2,1,0:T(2,128)(2,1)S(1)}, u32[]{:S(2)}, u32[]{:S(2)}) async-start(bf16[16,2,2,1024]{3,2,1,0:T(2,128)(2,1)} %copy.107), calls=%async_computation.4 | async-start | bytes 262144 | tf_op jit(solution)/shard_map/all_to_all | solution.py:104
  22.8 1.2 convolution_convert_fusion.1
  25.0 7.0 %all-to-all-done.4 = bf16[16,2,2,1024]{3,2,1,0:T(2,128)(2,1)S(1)} async-done(((bf16[16,2,2,1024]{3,2,1,0:T(2,128)(2,1)}), bf16[16,2,2,1024]{3,2,1,0:T(2,128)(2,1)S(1)}, u32[]{:S(2)}, u32[]{:S(2)}) %all-to-all-start.4) | async-done | bytes 131104 | tf_op jit(solution)/shard_map/all_to_all | solution.py:104
  32.0 3.5 all-to-all-start.9
  35.4 1.6 copy.98
  37.1 1.3 copy.99
  38.4 13.9 %all-to-all-done.9 = bf16[16,2,64,128]{3,2,1,0:T(8,128)(2,1)S(1)} async-done(((bf16[16,2,64,128]{3,2,1,0:T(8,128)(2,1)}), bf16[16,2,64,128]{3,2,1,0:T(8,128)(2,1)S(1)}, u32[]{:S(2)}, u32[]{:S(2)}) %all-to-all-start.9) | async-done | bytes 524320 | tf_op jit(solution)/shard_map/all_to_all | solution.py:103
  52.3 9.7 %all-to-all-start = ((bf16[128,32,1,128]{3,0,2,1:T(8,128)(2,1)}), bf16[128,32,1,128]{3,0,2,1:T(8,128)(2,1)S(1)}, u32[]{:S(2)}, u32[]{:S(2)}) async-start(bf16[128,32,1,128]{3,0,2,1:T(8,128)(2,1)} %copy.99), calls=%async_computation | async-start | bytes 2097152 | tf_op jit(solution)/shard_map/all_to_all | solution.py:152
  62.1 28.1 %all-to-all-done = bf16[128,32,1,128]{3,0,2,1:T(8,128)(2,1)S(1)} async-done(((bf16[128,32,1,128]{3,0,2,1:T(8,128)(2,1)}), bf16[128,32,1,128]{3,0,2,1:T(8,128)(2,1)S(1)}, u32[]{:S(2)}, u32[]{:S(2)}) %all-to-all-start) | async-done | bytes 1048608 | tf_op jit(solution)/shard_map/all_to_all | solution.py:152
  90.2 1.4 broadcast_in_dim.41
  91.6 5.5 all-to-all-start.1
  97.0 1.6 copy.101
  98.6 1.3 copy.102
  100.0 22.3 %all-to-all-done.1 = bf16[128,32,1,128]{3,0,2,1:T(8,128)(2,1)S(1)} async-done(((bf16[128,32,1,128]{3,0,2,1:T(8,128)(2,1)}), bf16[128,32,1,128]{3,0,2,1:T(8,128)(2,1)S(1)}, u32[]{:S(2)}, u32[]{:S(2)}) %all-to-all-start.1) | async-done | bytes 1048608 | tf_op jit(solution)/shard_map/all_to_all | solution.py:153
  122.2 8.1 %all-to-all-start.2 = ((bf16[128,32,1,128]{3,0,2,1:T(8,128)(2,1)}), bf16[128,32,1,128]{3,0,2,1:T(8,128)(2,1)}, u32[]{:S(2)}, u32[]{:S(2)}) async-start(bf16[128,32,1,128]{3,0,2,1:T(8,128)(2,1)} %copy.102), calls=%async_computation.2 | async-start | bytes 2097152 | tf_op jit(solution)/shard_map/all_to_all | solution.py:154
  131.2 1.6 copy.110
  132.9 1.3 copy.111
  135.8 19.1 %all-to-all-done.2 = bf16[128,32,1,128]{3,0,2,1:T(8,128)(2,1)} async-done(((bf16[128,32,1,128]{3,0,2,1:T(8,128)(2,1)}), bf16[128,32,1,128]{3,0,2,1:T(8,128)(2,1)}, u32[]{:S(2)}, u32[]{:S(2)}) %all-to-all-start.2) | async-done | bytes 1048608 | tf_op jit(solution)/shard_map/all_to_all | solution.py:154
  154.9 8.6 %all-to-all-start.7 = ((bf16[128,32,128]{2,0,1:T(8,128)(2,1)}), bf16[128,32,128]{2,0,1:T(8,128)(2,1)S(1)}, u32[]{:S(2)}, u32[]{:S(2)}) async-start(bf16[128,32,128]{2,0,1:T(8,128)(2,1)} %copy.111), calls=%async_computation.7 | async-start | bytes 2097152 | tf_op jit(solution)/shard_map/all_to_all | solution.py:131
  163.5 1.9 broadcast.204
  165.4 72.3 %while.19 = (s32[]{:T(128)}, f32[6144,128]{1,0:T(8,128)}, s32[8]{0:T(128)S(1)}, s32[6144]{0:T(1024)S(1)}, s32[4096]{0:T(1024)S(1)}, /*index=5*/bf16[4096,128]{1,...) while((s32[]{:T(128)}, f32[6144,128]{1,0:T(8,128)}, ...), condition=%wide.region_9.10_spmd, body=%wide.region_6.9_spmd.sunk | while | flops 685836288 | bytes 44509508 | solution.py:43
  166.8 2.6 fusion.60
  170.3 2.5 fusion.62
  172.8 1.7 copy-done.2
  175.9 2.6 fusion.60
  179.3 2.5 fusion.62
  181.8 1.7 copy-done.2
  184.9 2.6 fusion.60
  188.3 2.5 fusion.62
  190.8 1.7 copy-done.2
  193.9 2.6 fusion.60
  197.4 2.5 fusion.62
  199.9 1.7 copy-done.2
  203.0 2.6 fusion.60
  206.4 2.5 fusion.62
  208.9 1.7 copy-done.2
  212.0 2.6 fusion.60
  215.5 2.5 fusion.62
  218.0 1.7 copy-done.2
  221.1 2.6 fusion.60
  224.5 2.5 fusion.62
  227.0 1.7 copy-done.2
  230.1 2.6 fusion.60
  233.6 2.5 fusion.62
  236.1 1.7 copy-done.2
  237.7 1.7 fusion.9
  239.9 1.4 reduce.3
  242.5 9.2 %all-to-all-start.3 = ((bf16[32,2,8192]{2,1,0:T(2,128)(2,1)}), bf16[32,2,8192]{2,1,0:T(2,128)(2,1)S(1)}, u32[]{:S(2)}, u32[]{:S(2)}) async-start(bf16[32,2,8192]{2,1,0:T(2,128)(2,1)} %reshape.256), calls=%async_computation.3 | async-start | bytes 2097152 | tf_op jit(solution)/shard_map/all_to_all | solution.py:166
  252.0 1.9 convolution_bitcast_fusion
  256.0 20.3 %all-to-all-done.3 = bf16[32,2,8192]{2,1,0:T(2,128)(2,1)S(1)} async-done(((bf16[32,2,8192]{2,1,0:T(2,128)(2,1)}), bf16[32,2,8192]{2,1,0:T(2,128)(2,1)S(1)}, u32[]{:S(2)}, u32[]{:S(2)}) %all-to-all-start.3) | async-done | bytes 1048608 | tf_op jit(solution)/shard_map/all_to_all | solution.py:166
  277.3 8.4 %all-to-all-start.5 = ((bf16[32,2,1024]{2,1,0:T(2,128)(2,1)}), bf16[32,2,1024]{2,1,0:T(2,128)(2,1)S(1)}, u32[]{:S(2)}, u32[]{:S(2)}) async-start(bf16[32,2,1024]{2,1,0:T(2,128)(2,1)} %copy.109), calls=%async_computation.5 | async-start | bytes 262144 | tf_op jit(solution)/shard_map/all_to_all | solution.py:146
  285.7 4.3 reshape.257
  291.2 1.4 reduce_sum.74
  292.7 176.4 %reduce-scatter.2.cloned.1.call-done = f32[128,64]{0,1:T(8,128)} async-done(((f32[4096,64]{0,1:T(8,128)}), f32[128,64]{0,1:T(8,128)}) %reduce-scatter.2.cloned.1.call-update) | async-done | bytes 32784 | tf_op jit(solution)/shard_map/reduce_scatter | solution.py:135
  471.1 6.6 %all-to-all-start.10 = ((f32[1,64,1024]{2,0,1:T(1,128)}), f32[1,64,1024]{2,0,1:T(1,128)S(1)}, u32[]{:S(2)}, u32[]{:S(2)}) async-start(f32[1,64,1024]{2,0,1:T(1,128)} %copy.123), calls=%async_computation.11 | async-start | bytes 524288 | tf_op jit(solution)/shard_map/all_to_all | solution.py:189
  477.9 9.4 %all-to-all-done.10 = f32[1,64,1024]{2,0,1:T(1,128)S(1)} async-done(((f32[1,64,1024]{2,0,1:T(1,128)}), f32[1,64,1024]{2,0,1:T(1,128)S(1)}, u32[]{:S(2)}, u32[]{:S(2)}) %all-to-all-start.10) | async-done | bytes 262176 | tf_op jit(solution)/shard_map/all_to_all | solution.py:189
  488.3 4.4 all-to-all-start.6
  494.7 9.3 %all-to-all-done.6 = bf16[32,128,64]{1,2,0:T(8,128)(2,1)S(1)} async-done(((bf16[32,128,64]{1,2,0:T(8,128)(2,1)}), bf16[32,128,64]{1,2,0:T(8,128)(2,1)S(1)}, u32[]{:S(2)}, u32[]{:S(2)}) %all-to-all-start.6) | async-done | bytes 524320 | tf_op jit(solution)/shard_map/all_to_all | solution.py:182
  504.0 16.1 %all-to-all-start.11 = ((f32[16,2,2,1024]{3,1,2,0:T(2,128)}), f32[16,2,2,1024]{3,1,2,0:T(2,128)S(1)}, u32[]{:S(2)}, u32[]{:S(2)}) async-start(f32[16,2,2,1024]{3,1,2,0:T(2,128)} %copy.125), calls=%async_computation.12 | async-start | bytes 524288 | tf_op jit(solution)/shard_map/all_to_all | solution.py:201
  520.5 1.3 fusion.14
  521.9 1.5 copy.114
  523.4 8.4 %all-to-all-done.11 = f32[16,2,2,1024]{3,1,2,0:T(2,128)S(1)} async-done(((f32[16,2,2,1024]{3,1,2,0:T(2,128)}), f32[16,2,2,1024]{3,1,2,0:T(2,128)S(1)}, u32[]{:S(2)}, u32[]{:S(2)}) %all-to-all-start.11) | async-done | bytes 262176 | tf_op jit(solution)/shard_map/all_to_all | solution.py:201
  531.8 3.6 all-to-all-start.8
  536.6 26.0 %all-to-all-done.8 = f32[16,2,64,128]{3,1,2,0:T(2,128)S(1)} async-done(((f32[16,2,64,128]{3,1,2,0:T(2,128)}), f32[16,2,64,128]{3,1,2,0:T(2,128)S(1)}, u32[]{:S(2)}, u32[]{:S(2)}) %all-to-all-start.8) | async-done | bytes 1048608 | tf_op jit(solution)/shard_map/all_to_all | solution.py:194
  (135 shorter events, 35.6 us)
Async XLA Ops:
  7.2 54.8 %copy-start = (bf16[128,1024]{1,0:T(8,128)(2,1)S(1)}, bf16[128,1024]{1,0:T(8,128)(2,1)}, u32[]{:S(2)}) copy-start(bf16[128,1024]{1,0:T(8,128)(2,1)} %param.13) | copy-start | bytes 786436
  11.0 21.0 %all-to-all-start.4 = ((bf16[16,2,2,1024]{3,2,1,0:T(2,128)(2,1)}), bf16[16,2,2,1024]{3,2,1,0:T(2,128)(2,1)S(1)}, u32[]{:S(2)}, u32[]{:S(2)}) async-start(bf16[16,2,2,1024]{3,2,1,0:T(2,128)(2,1)} %copy.107), calls=%async_computation.4 | async-start | bytes 262144 | tf_op jit(solution)/shard_map/all_to_all | solution.py:104
  32.0 20.3 %all-to-all-start.9 = ((bf16[16,2,64,128]{3,2,1,0:T(8,128)(2,1)}), bf16[16,2,64,128]{3,2,1,0:T(8,128)(2,1)S(1)}, u32[]{:S(2)}, u32[]{:S(2)}) async-start(bf16[16,2,64,128]{3,2,1,0:T(8,128)(2,1)} %copy.119), calls=%async_computation.9 | async-start | bytes 1048576 | tf_op jit(solution)/shard_map/all_to_all | solution.py:103
  52.3 37.9 %all-to-all-start = ((bf16[128,32,1,128]{3,0,2,1:T(8,128)(2,1)}), bf16[128,32,1,128]{3,0,2,1:T(8,128)(2,1)S(1)}, u32[]{:S(2)}, u32[]{:S(2)}) async-start(bf16[128,32,1,128]{3,0,2,1:T(8,128)(2,1)} %copy.99), calls=%async_computation | async-start | bytes 2097152 | tf_op jit(solution)/shard_map/all_to_all | solution.py:152
  90.2 1.4 copy-start.4
  91.6 30.7 %all-to-all-start.1 = ((bf16[128,32,1,128]{3,0,2,1:T(8,128)(2,1)}), bf16[128,32,1,128]{3,0,2,1:T(8,128)(2,1)S(1)}, u32[]{:S(2)}, u32[]{:S(2)}) async-start(bf16[128,32,1,128]{3,0,2,1:T(8,128)(2,1)} %bitcast.10), calls=%async_computation.1 | async-start | bytes 2097152 | tf_op jit(solution)/shard_map/all_to_all | solution.py:153
  122.2 32.7 %all-to-all-start.2 = ((bf16[128,32,1,128]{3,0,2,1:T(8,128)(2,1)}), bf16[128,32,1,128]{3,0,2,1:T(8,128)(2,1)}, u32[]{:S(2)}, u32[]{:S(2)}) async-start(bf16[128,32,1,128]{3,0,2,1:T(8,128)(2,1)} %copy.102), calls=%async_computation.2 | async-start | bytes 2097152 | tf_op jit(solution)/shard_map/all_to_all | solution.py:154
  134.5 30.9 %copy-start.5 = (s32[32]{0:T(128)}, s32[32]{0:T(128)S(1)}, u32[]{:S(2)}) copy-start(s32[32]{0:T(128)S(1)} %select_reduce_fusion.1) | copy-start | bytes 388
  154.9 87.6 %all-to-all-start.7 = ((bf16[128,32,128]{2,0,1:T(8,128)(2,1)}), bf16[128,32,128]{2,0,1:T(8,128)(2,1)S(1)}, u32[]{:S(2)}, u32[]{:S(2)}) async-start(bf16[128,32,128]{2,0,1:T(8,128)(2,1)} %copy.111), calls=%async_computation.7 | async-start | bytes 2097152 | tf_op jit(solution)/shard_map/all_to_all | solution.py:131
  166.8 3.4 copy-start.1
  172.7 1.7 copy-start.2
  175.9 3.4 copy-start.1
  181.8 1.7 copy-start.2
  184.9 3.4 copy-start.1
  190.8 1.7 copy-start.2
  193.9 3.4 copy-start.1
  199.9 1.7 copy-start.2
  203.0 3.4 copy-start.1
  208.9 1.7 copy-start.2
  212.0 3.4 copy-start.1
  218.0 1.7 copy-start.2
  221.1 3.4 copy-start.1
  227.0 1.7 copy-start.2
  230.1 3.4 copy-start.1
  236.0 1.7 copy-start.2
  242.5 12.4 %copy-start.6 = (s32[32]{0:T(128)S(1)}, s32[32]{0:T(128)}, u32[]{:S(2)}) copy-start(s32[32]{0:T(128)} %copy-done.5) | copy-start | bytes 388
  242.5 33.7 %all-to-all-start.3 = ((bf16[32,2,8192]{2,1,0:T(2,128)(2,1)}), bf16[32,2,8192]{2,1,0:T(2,128)(2,1)S(1)}, u32[]{:S(2)}, u32[]{:S(2)}) async-start(bf16[32,2,8192]{2,1,0:T(2,128)(2,1)} %reshape.256), calls=%async_computation.3 | async-start | bytes 2097152 | tf_op jit(solution)/shard_map/all_to_all | solution.py:166
  251.8 217.4 %reduce-scatter.2.cloned.1.call-start = ((), (), s32[]{:S(2)}) async-start(), calls=%async_computation.13 | async-start | bytes 1081344 | tf_op jit(solution)/shard_map/reduce_scatter | solution.py:135
  276.2 1.0 copy-start.3
  277.3 193.8 %all-to-all-start.5 = ((bf16[32,2,1024]{2,1,0:T(2,128)(2,1)}), bf16[32,2,1024]{2,1,0:T(2,128)(2,1)S(1)}, u32[]{:S(2)}, u32[]{:S(2)}) async-start(bf16[32,2,1024]{2,1,0:T(2,128)(2,1)} %copy.109), calls=%async_computation.5 | async-start | bytes 262144 | tf_op jit(solution)/shard_map/all_to_all | solution.py:146
  291.2 202.3 %copy-start.7 = (s32[32]{0:T(128)S(1)}, s32[32]{0:T(128)}, u32[]{:S(2)}) copy-start(s32[32]{0:T(128)} %copy-done.5) | copy-start | bytes 388
  471.1 16.2 %all-to-all-start.10 = ((f32[1,64,1024]{2,0,1:T(1,128)}), f32[1,64,1024]{2,0,1:T(1,128)S(1)}, u32[]{:S(2)}, u32[]{:S(2)}) async-start(f32[1,64,1024]{2,0,1:T(1,128)} %copy.123), calls=%async_computation.11 | async-start | bytes 524288 | tf_op jit(solution)/shard_map/all_to_all | solution.py:189
  488.3 15.8 %all-to-all-start.6 = ((bf16[32,128,64]{1,2,0:T(8,128)(2,1)}), bf16[32,128,64]{1,2,0:T(8,128)(2,1)S(1)}, u32[]{:S(2)}, u32[]{:S(2)}) async-start(bf16[32,128,64]{1,2,0:T(8,128)(2,1)} %stack.3), calls=%async_computation.6 | async-start | bytes 1048576 | tf_op jit(solution)/shard_map/all_to_all | solution.py:182
  504.0 27.8 %all-to-all-start.11 = ((f32[16,2,2,1024]{3,1,2,0:T(2,128)}), f32[16,2,2,1024]{3,1,2,0:T(2,128)S(1)}, u32[]{:S(2)}, u32[]{:S(2)}) async-start(f32[16,2,2,1024]{3,1,2,0:T(2,128)} %copy.125), calls=%async_computation.12 | async-start | bytes 524288 | tf_op jit(solution)/shard_map/all_to_all | solution.py:201
  531.8 30.8 %all-to-all-start.8 = ((f32[16,2,64,128]{3,1,2,0:T(2,128)}), f32[16,2,64,128]{3,1,2,0:T(2,128)S(1)}, u32[]{:S(2)}, u32[]{:S(2)}) async-start(f32[16,2,64,128]{3,1,2,0:T(2,128)} %copy.114), calls=%async_computation.8 | async-start | bytes 2097152 | tf_op jit(solution)/shard_map/all_to_all | solution.py:194
Sparse Core Ops, SparseCore 0:
  257.0 212.1 reduce-scatter.1
